TPU v7x, 512 devices: a whole 4x4x16 slice. The times are simulated.
512 devices in a mesh: rows: 32 (over x, y, core), upd: 16 (over z).
Axes of the slice: x: 4, y: 4, z: 16, core: 2. Of those that a mesh axis runs over, the one named last changes fastest.
Arguments:
- tile_factors: bfloat16 [32, 128, 1024, 128], P('rows', 'upd'), may hold values from -6 to 6
- panel_factors: bfloat16 [128, 1024, 128], P('upd', 'rows'), may hold values from -0.1875 to 0.1875
- nonnull: int32 [32, 128], P('rows', 'upd'), may hold values from 0 to 1, as said below
- sketch: float32 [64, 1024], replicated, may hold values from -6 to 6
Outputs:
- update_factors: float32 [32, 1024, 128], P('rows', 'upd')
Inputs may be any that keep to these rules, and one draw needn't show every extreme that they name: In every aligned block of 8 update indices the first one is nonnull for every tile row.
All inputs are finite; a program needn't handle non-finite values.
Results may differ from a plain program's by a relative error of at most 0.0003.
Values may be sent and summed in bfloat16 or wider, within the bound.
No kernel may reach another device: no remote copies, remote signals or barrier semaphores. Data moves between devices by JAX's collectives and lax.ppermute only.
A program may use at most 64 MiB of HBM per device.

v0:
```python
import jax
import jax.numpy as jnp
from jax import lax
from jax.sharding import PartitionSpec as P


def from_partner(shard, axis, stride):
    return lax.ppermute(shard, axis, [(i, i ^ 1 << stride) for i in range(lax.axis_size(axis))])


def compress(lefts, rights, sketch):
    hi = lax.Precision.HIGHEST
    proj = jnp.einsum("nbr,sb->nrs", rights, sketch, precision=hi)
    span = jnp.einsum("nbr,nrs->bs", lefts, proj, precision=hi)
    gram = jnp.dot(span.T, span, precision=hi)
    order = gram.shape[0]
    shift = 0.001 * jnp.trace(gram) / order + 1e-20
    gram = gram + shift * jnp.eye(order, dtype=gram.dtype)
    chol = jnp.linalg.cholesky(gram)
    basis = lax.linalg.triangular_solve(chol, span, left_side=False, lower=True, transpose_a=True)
    coef = jnp.einsum("nbr,bs->nrs", lefts, basis, precision=hi)
    image = jnp.einsum("nbr,nrs->bs", rights, coef, precision=hi)
    return (basis, image)


def merge_pair(pair, sketch, rank):
    basis, image = compress(pair[:, :, :rank], pair[:, :, rank:], sketch)
    return jnp.concatenate([basis, image], axis=-1)


def body(tile_factors, panel_factors, nonnull, sketch):
    rank = tile_factors.shape[3] // 2
    tiles = tile_factors[0]
    own_right = tiles[:, :, rank:]
    panel = lax.all_gather(panel_factors, "rows", axis=1, tiled=True)
    inner = jnp.einsum(
        "kbr,kbs->krs", own_right, panel[:, :, rank:], preferred_element_type=jnp.float32
    )
    far_left = panel[:, :, :rank]
    weight = nonnull[0].astype(jnp.float32)
    lefts = jnp.einsum(
        "kbr,krs->kbs",
        tiles[:, :, :rank].astype(jnp.float32),
        inner,
        precision=lax.Precision.HIGHEST,
    )
    lefts = lefts * weight[:, None, None]
    basis, image = compress(lefts, far_left.astype(jnp.float32), sketch)
    packed = jnp.concatenate([basis, image], axis=-1)
    levels = lax.axis_size("upd").bit_length() - 1
    for level in range(levels):
        other = from_partner(packed, "upd", level)
        upper = lax.axis_index("upd") >> level & 1 == 1
        low = jnp.where(upper, other, packed)
        high = jnp.where(upper, packed, other)
        packed = merge_pair(jnp.stack([low, high]), sketch, rank)
    scale = jnp.float32(packed.shape[0]) ** 0.5
    result = jnp.concatenate([packed[:, :rank] * scale, packed[:, rank:] / scale], axis=-1)
    share = packed.shape[0] // lax.axis_size("upd")
    mine = lax.dynamic_slice_in_dim(result, lax.axis_index("upd") * share, share, 0)
    return mine[None]


def solution(mesh):
    in_specs = (P("rows", "upd", None, None), P("upd", "rows", None), P("rows", "upd"), P())
    out_specs = P("rows", "upd", None)
    return jax.shard_map(body, mesh=mesh, in_specs=in_specs, out_specs=out_specs, check_vma=False)
```

profile of v0, /device:TPU:1, one launch (start us, length us, event | category | flops | bytes accessed | tf_op | source)
XLA Modules:
  0.0 328.8 jit_solution(11202653416886925605)
XLA Ops:
  6.5 1.5 copy.41
  8.1 2.9 copy.40
  11.0 64.0 %all-gather.2.cloned.1.call-done = bf16[8,1024,128]{2,0,1:T(8,128)(2,1)} async-done(((bf16[8,32,128]{2,0,1:T(8,128)(2,1)}), bf16[8,1024,128]{2,0,1:T(8,128)(2,1)}) %all-gather.2.cloned.1.call-update) | async-done | bytes 2097168 | tf_op jit(solution)/shard_map/all_gather | solution.py:35
  75.1 4.3 %fusion.93 = (bf16[8,1024,64]{2,0,1:T(8,128)(2,1)}, bf16[8,1024,64]{2,0,1:T(8,128)(2,1)S(1)}) fusion(bf16[8,1024,128]{2,0,1:T(8,128)(2,1)} %all-gather.2.cloned.1.call-done), kind=kLoop, calls=%fused_computation.149 | loop fusion | bytes 4194304 | tf_op jit(solution)/shard_map/slice | solution.py:39
  80.1 2.2 fusion.12
  82.3 2.5 copy.88
  84.9 1.6 fusion.38
  86.5 1.6 fusion.8
  90.5 5.8 %cholesky.89 = f32[64,64]{1,0:T(8,128)S(1)} custom-call(f32[64,64]{1,0:T(8,128)S(1)} %fusion.68), custom_call_target="Cholesky" | custom-call | tf_op jit(solution)/shard_map/jit(cholesky)/cholesky | solution.py:19
  97.7 4.9 %custom-call.9 = f32[1,64,64]{1,2,0:T(8,128)S(1)} custom-call(f32[1,64,64]{2,1,0:T(8,128)S(1)} %fusion.49), custom_call_target="InvertDiagBlocksLowerTriangular" | custom-call | tf_op jit(solution)/shard_map/triangular_solve/custom-call.0 | solution.py:20
  102.6 1.4 fusion.66
  104.0 3.2 fusion.2
  108.0 3.4 %collective-permute-start = (f32[1024,128]{0,1:T(8,128)S(1)}, f32[1024,128]{0,1:T(8,128)S(1)}, u32[]{:S(2)}, u32[]{:S(2)}) collective-permute-start(f32[1024,128]{0,1:T(8,128)S(1)} %pad_maximum_fusion.4), channel_id=1, source_target_pairs={{0,1},{1,0},{2,3},{3,2},{4,5},{5,4},{6,7},{7,6},{8,9},{9,8},{10,11... | collective-permute-start | bytes 1572872 | tf_op jit(solution)/shard_map/ppermute | solution.py:8
  111.4 11.7 %collective-permute-done = f32[1024,128]{0,1:T(8,128)S(1)} collective-permute-done((f32[1024,128]{0,1:T(8,128)S(1)}, f32[1024,128]{0,1:T(8,128)S(1)}, u32[]{:S(2)}, u32[]{:S(2)}) %collective-permute-start) | collective-permute-done | bytes 524320 | tf_op jit(solution)/shard_map/ppermute | solution.py:8
  123.1 1.1 select_bitcast_fusion.7
  125.5 1.0 select_reduce_fusion.4
  127.2 5.8 %cholesky.100 = f32[64,64]{1,0:T(8,128)S(1)} custom-call(f32[64,64]{1,0:T(8,128)S(1)} %fusion.65), custom_call_target="Cholesky" | custom-call | tf_op jit(solution)/shard_map/jit(cholesky)/cholesky | solution.py:19
  134.4 4.9 %custom-call.10 = f32[1,64,64]{1,2,0:T(8,128)S(1)} custom-call(f32[1,64,64]{2,1,0:T(8,128)S(1)} %fusion.50), custom_call_target="InvertDiagBlocksLowerTriangular" | custom-call | tf_op jit(solution)/shard_map/triangular_solve/custom-call.0 | solution.py:20
  141.1 4.2 %collective-permute-start.1 = (f32[1024,128]{0,1:T(8,128)S(1)}, f32[1024,128]{0,1:T(8,128)S(1)}, u32[]{:S(2)}, u32[]{:S(2)}) collective-permute-start(f32[1024,128]{0,1:T(8,128)S(1)} %pad_maximum_fusion.5), channel_id=1, source_target_pairs={{0,2},{1,3},{2,0},{3,1},{4,6},{5,7},{6,4},{7,5},{8,10},{9,11},{10,... | collective-permute-start | bytes 1572872 | tf_op jit(solution)/shard_map/ppermute | solution.py:8
  145.3 22.7 %collective-permute-done.1 = f32[1024,128]{0,1:T(8,128)S(1)} collective-permute-done((f32[1024,128]{0,1:T(8,128)S(1)}, f32[1024,128]{0,1:T(8,128)S(1)}, u32[]{:S(2)}, u32[]{:S(2)}) %collective-permute-start.1) | collective-permute-done | bytes 524320 | tf_op jit(solution)/shard_map/ppermute | solution.py:8
  171.2 5.8 %cholesky.111 = f32[64,64]{1,0:T(8,128)S(1)} custom-call(f32[64,64]{1,0:T(8,128)S(1)} %fusion.62), custom_call_target="Cholesky" | custom-call | tf_op jit(solution)/shard_map/jit(cholesky)/cholesky | solution.py:19
  178.4 4.9 %custom-call.11 = f32[1,64,64]{1,2,0:T(8,128)S(1)} custom-call(f32[1,64,64]{2,1,0:T(8,128)S(1)} %fusion.51), custom_call_target="InvertDiagBlocksLowerTriangular" | custom-call | tf_op jit(solution)/shard_map/triangular_solve/custom-call.0 | solution.py:20
  185.1 7.6 %collective-permute-start.2 = (f32[1024,128]{0,1:T(8,128)S(1)}, f32[1024,128]{0,1:T(8,128)S(1)}, u32[]{:S(2)}, u32[]{:S(2)}) collective-permute-start(f32[1024,128]{0,1:T(8,128)S(1)} %pad_maximum_fusion.6), channel_id=1, source_target_pairs={{0,4},{1,5},{2,6},{3,7},{4,0},{5,1},{6,2},{7,3},{8,12},{9,13},{10,... | collective-permute-start | bytes 1572872 | tf_op jit(solution)/shard_map/ppermute | solution.py:8
  192.7 44.8 %collective-permute-done.2 = f32[1024,128]{0,1:T(8,128)S(1)} collective-permute-done((f32[1024,128]{0,1:T(8,128)S(1)}, f32[1024,128]{0,1:T(8,128)S(1)}, u32[]{:S(2)}, u32[]{:S(2)}) %collective-permute-start.2) | collective-permute-done | bytes 524320 | tf_op jit(solution)/shard_map/ppermute | solution.py:8
  239.0 1.0 select_reduce_fusion.2
  240.7 5.8 %cholesky.122 = f32[64,64]{1,0:T(8,128)S(1)} custom-call(f32[64,64]{1,0:T(8,128)S(1)} %fusion.59), custom_call_target="Cholesky" | custom-call | tf_op jit(solution)/shard_map/jit(cholesky)/cholesky | solution.py:19
  247.9 4.9 %custom-call.12 = f32[1,64,64]{1,2,0:T(8,128)S(1)} custom-call(f32[1,64,64]{2,1,0:T(8,128)S(1)} %fusion.52), custom_call_target="InvertDiagBlocksLowerTriangular" | custom-call | tf_op jit(solution)/shard_map/triangular_solve/custom-call.0 | solution.py:20
  254.6 11.1 %collective-permute-start.3 = (f32[1024,128]{0,1:T(8,128)S(1)}, f32[1024,128]{0,1:T(8,128)S(1)}, u32[]{:S(2)}, u32[]{:S(2)}) collective-permute-start(f32[1024,128]{0,1:T(8,128)S(1)} %pad_maximum_fusion.7), channel_id=1, source_target_pairs={{0,8},{1,9},{2,10},{3,11},{4,12},{5,13},{6,14},{7,15},{8,0},{9,1},... | collective-permute-start | bytes 1572872 | tf_op jit(solution)/shard_map/ppermute | solution.py:8
  265.7 38.4 %collective-permute-done.3 = f32[1024,128]{0,1:T(8,128)S(1)} collective-permute-done((f32[1024,128]{0,1:T(8,128)S(1)}, f32[1024,128]{0,1:T(8,128)S(1)}, u32[]{:S(2)}, u32[]{:S(2)}) %collective-permute-start.3) | collective-permute-done | bytes 524320 | tf_op jit(solution)/shard_map/ppermute | solution.py:8
  305.6 1.0 select_reduce_fusion.1
  307.3 5.8 %cholesky.133 = f32[64,64]{1,0:T(8,128)S(1)} custom-call(f32[64,64]{1,0:T(8,128)S(1)} %fusion.56), custom_call_target="Cholesky" | custom-call | tf_op jit(solution)/shard_map/jit(cholesky)/cholesky | solution.py:19
  314.5 4.9 %custom-call.13 = f32[1,64,64]{1,2,0:T(8,128)S(1)} custom-call(f32[1,64,64]{2,1,0:T(8,128)S(1)} %fusion.53), custom_call_target="InvertDiagBlocksLowerTriangular" | custom-call | tf_op jit(solution)/shard_map/triangular_solve/custom-call.0 | solution.py:20
  (76 shorter events, 24.8 us)
Async XLA Ops:
  6.5 78.3 %copy-start = (f32[64,1024]{1,0:T(8,128)S(1)}, f32[64,1024]{1,0:T(8,128)}, u32[]{:S(2)}) copy-start(f32[64,1024]{1,0:T(8,128)} %param.10) | copy-start | bytes 786436
  6.5 68.5 %all-gather.2.cloned.1.call-start = ((), (), s32[]{:S(2)}) async-start(), calls=%async_computation | async-start | bytes 2162688 | tf_op jit(solution)/shard_map/all_gather | solution.py:35
  8.1 2.9 copy-start.4
  11.0 68.4 %copy-start.1 = (bf16[1,8,1024,128]{2,3,1,0:T(8,128)(2,1)}, bf16[1,8,1024,128]{2,3,1,0:T(8,128)(2,1)S(1)}, u32[]{:S(2)}) copy-start(bf16[1,8,1024,128]{2,3,1,0:T(8,128)(2,1)S(1)} %copy.40) | copy-start | bytes 6291460
  88.1 0.7 copy-start.2
  104.0 4.0 %copy-start.3 = (f32[64,1024]{1,0:T(8,128)}, f32[64,1024]{1,0:T(8,128)S(1)}, u32[]{:S(2)}) copy-start(f32[64,1024]{1,0:T(8,128)S(1)} %fusion.66) | copy-start | bytes 786436
  108.0 15.1 %collective-permute-start = (f32[1024,128]{0,1:T(8,128)S(1)}, f32[1024,128]{0,1:T(8,128)S(1)}, u32[]{:S(2)}, u32[]{:S(2)}) collective-permute-start(f32[1024,128]{0,1:T(8,128)S(1)} %pad_maximum_fusion.4), channel_id=1, source_target_pairs={{0,1},{1,0},{2,3},{3,2},{4,5},{5,4},{6,7},{7,6},{8,9},{9,8},{10,11... | collective-permute-start | bytes 1572872 | tf_op jit(solution)/shard_map/ppermute | solution.py:8
  141.1 26.9 %collective-permute-start.1 = (f32[1024,128]{0,1:T(8,128)S(1)}, f32[1024,128]{0,1:T(8,128)S(1)}, u32[]{:S(2)}, u32[]{:S(2)}) collective-permute-start(f32[1024,128]{0,1:T(8,128)S(1)} %pad_maximum_fusion.5), channel_id=1, source_target_pairs={{0,2},{1,3},{2,0},{3,1},{4,6},{5,7},{6,4},{7,5},{8,10},{9,11},{10,... | collective-permute-start | bytes 1572872 | tf_op jit(solution)/shard_map/ppermute | solution.py:8
  185.1 52.5 %collective-permute-start.2 = (f32[1024,128]{0,1:T(8,128)S(1)}, f32[1024,128]{0,1:T(8,128)S(1)}, u32[]{:S(2)}, u32[]{:S(2)}) collective-permute-start(f32[1024,128]{0,1:T(8,128)S(1)} %pad_maximum_fusion.6), channel_id=1, source_target_pairs={{0,4},{1,5},{2,6},{3,7},{4,0},{5,1},{6,2},{7,3},{8,12},{9,13},{10,... | collective-permute-start | bytes 1572872 | tf_op jit(solution)/shard_map/ppermute | solution.py:8
  254.6 49.5 %collective-permute-start.3 = (f32[1024,128]{0,1:T(8,128)S(1)}, f32[1024,128]{0,1:T(8,128)S(1)}, u32[]{:S(2)}, u32[]{:S(2)}) collective-permute-start(f32[1024,128]{0,1:T(8,128)S(1)} %pad_maximum_fusion.7), channel_id=1, source_target_pairs={{0,8},{1,9},{2,10},{3,11},{4,12},{5,13},{6,14},{7,15},{8,0},{9,1},... | collective-permute-start | bytes 1572872 | tf_op jit(solution)/shard_map/ppermute | solution.py:8
Sparse Core Ops, SparseCore 0:
  10.5 64.5 all-gather.1
where the time goes:
time: 329 us
  waiting for transfers between devices  182 us (55%)
  other arithmetic  62.1 us (19%)
  matrix products  28.6 us (9%)
  starting transfers between devices  26.3 us (8%)
  between operations  17.1 us (5%)
  local copies, waits for them, and re-layouts  13 us (4%)
    ppermute x4, waiting for transfers between devices, from_partner(): lax.ppermute(shard, axis, [(i, i ^ 1 << stride) for i in range(lax.axis_s...  118 us
    all_gather x1, waiting for transfers between devices, body(): panel = lax.all_gather(panel_factors, 'rows', axis=1, tiled=True)  64 us
    another operation x15, other arithmetic, compress(): chol = jnp.linalg.cholesky(gram)  32.6 us
    another operation x10, other arithmetic, compress(): lax.linalg.triangular_solve(chol, span, left_side=False, lower=True, tran...  27.7 us
    ppermute x4, starting transfers between devices, from_partner(): lax.ppermute(shard, axis, [(i, i ^ 1 << stride) for i in range(lax.axis_s...  26.3 us
    unnamed x13, local copies, waits for them, and re-layouts  7.62 us
    dot_general x5, matrix products, compress(): coef = jnp.einsum('nbr,bs->nrs', lefts, basis, precision=hi)  6.75 us
  transfers between devices with their start and end apart: 5, of which 5 were waited for; matrix products, arithmetic and copies ran while one was open for 1% of the time, Pallas kernels for 0%

commit v1 on v0

--- a/solution.py
+++ b/solution.py
@@ -32,7 +32,9 @@
     rank = tile_factors.shape[3] // 2
     tiles = tile_factors[0]
     own_right = tiles[:, :, rank:]
-    panel = lax.all_gather(panel_factors, "rows", axis=1, tiled=True)
+    panel = jnp.concatenate(
+        lax.all_to_all(jnp.stack([panel_factors] * lax.axis_size("rows")), "rows", 0, 0), axis=1
+    )
     inner = jnp.einsum(
         "kbr,kbs->krs", own_right, panel[:, :, rank:], preferred_element_type=jnp.float32
     )

time: 329 us -> 287 us (0.87)
  waiting for transfers between devices: 182 us -> 148 us
  between operations: 17.1 us -> 3.73 us
  starting transfers between devices: 26.3 us -> 34.4 us
  local copies, waits for them, and re-layouts: 13 us -> 8.57 us
    all_gather x1 -> x0, waiting for transfers between devices: 64 us -> none  [body(): panel = lax.all_gather(panel_factors, 'rows', axis=1, tiled=True)]
    all_to_all x0 -> x1, waiting for transfers between devices: none -> 25.8 us  [body(): lax.all_to_all(jnp.stack([panel_factors] * lax.axis_size('rows')), 'rows'...]
    all_to_all x0 -> x1, starting transfers between devices: none -> 11.3 us  [body(): lax.all_to_all(jnp.stack([panel_factors] * lax.axis_size('rows')), 'rows'...]
    unnamed x13 -> x11, local copies, waits for them, and re-layouts: 7.62 us -> 2.67 us
    ppermute x4, waiting for transfers between devices: 118 us -> 123 us  [from_partner(): lax.ppermute(shard, axis, [(i, i ^ 1 << stride) for i in range(lax.axis_s...]
    slice x1 -> x0, local copies, waits for them, and re-layouts: 4.28 us -> none  [body(): far_left = panel[:, :, :rank]]
where the time goes in v1:
time: 287 us; the launch traced here: 286 us
  waiting for transfers between devices  148 us (52%)
  other arithmetic  61.2 us (21%)
  starting transfers between devices  34.4 us (12%)
  matrix products  29.9 us (10%)
  local copies, waits for them, and re-layouts  8.57 us (3%)
  between operations  3.73 us (1%)
    ppermute x4, waiting for transfers between devices, from_partner(): lax.ppermute(shard, axis, [(i, i ^ 1 << stride) for i in range(lax.axis_s...  123 us
    another operation x15, other arithmetic, compress(): chol = jnp.linalg.cholesky(gram)  32.6 us
    another operation x10, other arithmetic, compress(): lax.linalg.triangular_solve(chol, span, left_side=False, lower=True, tran...  27.7 us
    all_to_all x1, waiting for transfers between devices, body(): lax.all_to_all(jnp.stack([panel_factors] * lax.axis_size('rows')), 'rows'...  25.8 us
    ppermute x4, starting transfers between devices, from_partner(): lax.ppermute(shard, axis, [(i, i ^ 1 << stride) for i in range(lax.axis_s...  23.1 us
    all_to_all x1, starting transfers between devices, body(): lax.all_to_all(jnp.stack([panel_factors] * lax.axis_size('rows')), 'rows'...  11.3 us
    dot_general x5, matrix products, compress(): coef = jnp.einsum('nbr,bs->nrs', lefts, basis, precision=hi)  8.34 us
  transfers between devices with their start and end apart: 5, of which 5 were waited for; matrix products, arithmetic and copies ran while one was open for 1% of the time, Pallas kernels for 0%

profile of v1, /device:TPU:1, one launch (start us, length us, event | category | flops | bytes accessed | tf_op | source)
XLA Modules:
  0.0 286.2 jit_solution(6937100170455171208)
XLA Ops:
  0.0 2.6 stack.26
  2.7 11.3 %all-to-all-start = ((bf16[32,8,32,128]{3,2,1,0:T(8,128)(2,1)}), bf16[32,8,32,128]{3,2,1,0:T(8,128)(2,1)}, u32[]{:S(2)}, u32[]{:S(2)}) async-start(bf16[32,8,32,128]{3,2,1,0:T(8,128)(2,1)} %stack.26), calls=%async_computation | async-start | bytes 4194304 | tf_op jit(solution)/shard_map/all_to_all | solution.py:36
  14.0 2.6 copy.40
  16.6 25.8 %all-to-all-done = bf16[32,8,32,128]{3,2,1,0:T(8,128)(2,1)} async-done(((bf16[32,8,32,128]{3,2,1,0:T(8,128)(2,1)}), bf16[32,8,32,128]{3,2,1,0:T(8,128)(2,1)}, u32[]{:S(2)}, u32[]{:S(2)}) %all-to-all-start) | async-done | bytes 2097184 | tf_op jit(solution)/shard_map/all_to_all | solution.py:36
  42.5 2.2 copy.41
  44.7 1.8 fusion
  46.5 1.0 fusion.19
  47.5 1.2 fusion.8
  48.7 1.6 fusion.15
  52.1 5.8 %cholesky.89 = f32[64,64]{1,0:T(8,128)S(1)} custom-call(f32[64,64]{1,0:T(8,128)S(1)} %fusion.74), custom_call_target="Cholesky" | custom-call | tf_op jit(solution)/shard_map/jit(cholesky)/cholesky | solution.py:19
  59.3 4.9 %custom-call.9 = f32[1,64,64]{1,2,0:T(8,128)S(1)} custom-call(f32[1,64,64]{2,1,0:T(8,128)S(1)} %fusion.55), custom_call_target="InvertDiagBlocksLowerTriangular" | custom-call | tf_op jit(solution)/shard_map/triangular_solve/custom-call.0 | solution.py:20
  64.6 4.8 %fusion.2 = f32[8,64,64]{1,2,0:T(8,128)S(1)} fusion(f32[8,64,1024]{2,1,0:T(8,128)} %copy-done.1, f32[8]{0:T(128)S(1)} %convert_bitcast_fusion, f32[64,1024]{1,0:T(8,128)S(1)} %fusion.72), kind=kOutput, calls=%fused_computation.2 | convolution fusion | flops 403177472 | bytes 2490400 | tf_op jit(solution)/shard_map/nbr,bs->nrs/dot_general | solution.py:21
  69.4 2.0 fusion.12
  71.5 2.1 collective-permute-start
  73.6 12.4 %collective-permute-done = f32[1024,128]{0,1:T(8,128)S(1)} collective-permute-done((f32[1024,128]{0,1:T(8,128)S(1)}, f32[1024,128]{0,1:T(8,128)S(1)}, u32[]{:S(2)}, u32[]{:S(2)}) %collective-permute-start) | collective-permute-done | bytes 524320 | tf_op jit(solution)/shard_map/ppermute | solution.py:8
  87.5 1.0 select_reduce_fusion.4
  89.2 5.8 %cholesky.100 = f32[64,64]{1,0:T(8,128)S(1)} custom-call(f32[64,64]{1,0:T(8,128)S(1)} %fusion.71), custom_call_target="Cholesky" | custom-call | tf_op jit(solution)/shard_map/jit(cholesky)/cholesky | solution.py:19
  96.4 4.9 %custom-call.10 = f32[1,64,64]{1,2,0:T(8,128)S(1)} custom-call(f32[1,64,64]{2,1,0:T(8,128)S(1)} %fusion.56), custom_call_target="InvertDiagBlocksLowerTriangular" | custom-call | tf_op jit(solution)/shard_map/triangular_solve/custom-call.0 | solution.py:20
  103.1 2.6 collective-permute-start.1
  105.7 25.2 %collective-permute-done.1 = f32[1024,128]{0,1:T(8,128)S(1)} collective-permute-done((f32[1024,128]{0,1:T(8,128)S(1)}, f32[1024,128]{0,1:T(8,128)S(1)}, u32[]{:S(2)}, u32[]{:S(2)}) %collective-permute-start.1) | collective-permute-done | bytes 524320 | tf_op jit(solution)/shard_map/ppermute | solution.py:8
  132.4 1.0 select_reduce_fusion.3
  134.1 5.8 %cholesky.111 = f32[64,64]{1,0:T(8,128)S(1)} custom-call(f32[64,64]{1,0:T(8,128)S(1)} %fusion.68), custom_call_target="Cholesky" | custom-call | tf_op jit(solution)/shard_map/jit(cholesky)/cholesky | solution.py:19
  141.3 4.9 %custom-call.11 = f32[1,64,64]{1,2,0:T(8,128)S(1)} custom-call(f32[1,64,64]{2,1,0:T(8,128)S(1)} %fusion.57), custom_call_target="InvertDiagBlocksLowerTriangular" | custom-call | tf_op jit(solution)/shard_map/triangular_solve/custom-call.0 | solution.py:20
  148.0 6.4 %collective-permute-start.2 = (f32[1024,128]{0,1:T(8,128)S(1)}, f32[1024,128]{0,1:T(8,128)S(1)}, u32[]{:S(2)}, u32[]{:S(2)}) collective-permute-start(f32[1024,128]{0,1:T(8,128)S(1)} %pad_maximum_fusion.6), channel_id=1, source_target_pairs={{0,4},{1,5},{2,6},{3,7},{4,0},{5,1},{6,2},{7,3},{8,12},{9,13},{10,... | collective-permute-start | bytes 1572872 | tf_op jit(solution)/shard_map/ppermute | solution.py:8
  154.5 45.9 %collective-permute-done.2 = f32[1024,128]{0,1:T(8,128)S(1)} collective-permute-done((f32[1024,128]{0,1:T(8,128)S(1)}, f32[1024,128]{0,1:T(8,128)S(1)}, u32[]{:S(2)}, u32[]{:S(2)}) %collective-permute-start.2) | collective-permute-done | bytes 524320 | tf_op jit(solution)/shard_map/ppermute | solution.py:8
  201.8 1.0 select_reduce_fusion.2
  203.6 5.8 %cholesky.122 = f32[64,64]{1,0:T(8,128)S(1)} custom-call(f32[64,64]{1,0:T(8,128)S(1)} %fusion.65), custom_call_target="Cholesky" | custom-call | tf_op jit(solution)/shard_map/jit(cholesky)/cholesky | solution.py:19
  210.7 4.9 %custom-call.12 = f32[1,64,64]{1,2,0:T(8,128)S(1)} custom-call(f32[1,64,64]{2,1,0:T(8,128)S(1)} %fusion.58), custom_call_target="InvertDiagBlocksLowerTriangular" | custom-call | tf_op jit(solution)/shard_map/triangular_solve/custom-call.0 | solution.py:20
  217.4 12.0 %collective-permute-start.3 = (f32[1024,128]{0,1:T(8,128)S(1)}, f32[1024,128]{0,1:T(8,128)S(1)}, u32[]{:S(2)}, u32[]{:S(2)}) collective-permute-start(f32[1024,128]{0,1:T(8,128)S(1)} %pad_maximum_fusion.7), channel_id=1, source_target_pairs={{0,8},{1,9},{2,10},{3,11},{4,12},{5,13},{6,14},{7,15},{8,0},{9,1},... | collective-permute-start | bytes 1572872 | tf_op jit(solution)/shard_map/ppermute | solution.py:8
  229.4 39.0 %collective-permute-done.3 = f32[1024,128]{0,1:T(8,128)S(1)} collective-permute-done((f32[1024,128]{0,1:T(8,128)S(1)}, f32[1024,128]{0,1:T(8,128)S(1)}, u32[]{:S(2)}, u32[]{:S(2)}) %collective-permute-start.3) | collective-permute-done | bytes 524320 | tf_op jit(solution)/shard_map/ppermute | solution.py:8
  271.6 5.8 %cholesky.133 = f32[64,64]{1,0:T(8,128)S(1)} custom-call(f32[64,64]{1,0:T(8,128)S(1)} %fusion.62), custom_call_target="Cholesky" | custom-call | tf_op jit(solution)/shard_map/jit(cholesky)/cholesky | solution.py:19
  278.7 4.9 %custom-call.13 = f32[1,64,64]{1,2,0:T(8,128)S(1)} custom-call(f32[1,64,64]{2,1,0:T(8,128)S(1)} %fusion.59), custom_call_target="InvertDiagBlocksLowerTriangular" | custom-call | tf_op jit(solution)/shard_map/triangular_solve/custom-call.0 | solution.py:20
  (74 shorter events, 23.2 us)
Async XLA Ops:
  0.0 47.5 %copy-start = (f32[64,1024]{1,0:T(8,128)S(1)}, f32[64,1024]{1,0:T(8,128)}, u32[]{:S(2)}) copy-start(f32[64,1024]{1,0:T(8,128)} %param.10) | copy-start | bytes 786436
  2.7 11.3 %copy-start.3 = (bf16[1,8,1024,128]{3,2,1,0:T(8,128)(2,1)S(1)}, bf16[1,8,1024,128]{3,2,1,0:T(8,128)(2,1)}, u32[]{:S(2)}) copy-start(bf16[1,8,1024,128]{3,2,1,0:T(8,128)(2,1)} %param.7) | copy-start | bytes 6291460
  2.7 39.8 %all-to-all-start = ((bf16[32,8,32,128]{3,2,1,0:T(8,128)(2,1)}), bf16[32,8,32,128]{3,2,1,0:T(8,128)(2,1)}, u32[]{:S(2)}, u32[]{:S(2)}) async-start(bf16[32,8,32,128]{3,2,1,0:T(8,128)(2,1)} %stack.26), calls=%async_computation | async-start | bytes 4194304 | tf_op jit(solution)/shard_map/all_to_all | solution.py:36
  14.0 2.6 copy-start.4
  42.4 2.2 copy-start.2
  47.5 2.8 copy-start.1
  71.5 14.6 %collective-permute-start = (f32[1024,128]{0,1:T(8,128)S(1)}, f32[1024,128]{0,1:T(8,128)S(1)}, u32[]{:S(2)}, u32[]{:S(2)}) collective-permute-start(f32[1024,128]{0,1:T(8,128)S(1)} %pad_maximum_fusion.4), channel_id=1, source_target_pairs={{0,1},{1,0},{2,3},{3,2},{4,5},{5,4},{6,7},{7,6},{8,9},{9,8},{10,11... | collective-permute-start | bytes 1572872 | tf_op jit(solution)/shard_map/ppermute | solution.py:8
  103.1 27.9 %collective-permute-start.1 = (f32[1024,128]{0,1:T(8,128)S(1)}, f32[1024,128]{0,1:T(8,128)S(1)}, u32[]{:S(2)}, u32[]{:S(2)}) collective-permute-start(f32[1024,128]{0,1:T(8,128)S(1)} %pad_maximum_fusion.5), channel_id=1, source_target_pairs={{0,2},{1,3},{2,0},{3,1},{4,6},{5,7},{6,4},{7,5},{8,10},{9,11},{10,... | collective-permute-start | bytes 1572872 | tf_op jit(solution)/shard_map/ppermute | solution.py:8
  148.0 52.3 %collective-permute-start.2 = (f32[1024,128]{0,1:T(8,128)S(1)}, f32[1024,128]{0,1:T(8,128)S(1)}, u32[]{:S(2)}, u32[]{:S(2)}) collective-permute-start(f32[1024,128]{0,1:T(8,128)S(1)} %pad_maximum_fusion.6), channel_id=1, source_target_pairs={{0,4},{1,5},{2,6},{3,7},{4,0},{5,1},{6,2},{7,3},{8,12},{9,13},{10,... | collective-permute-start | bytes 1572872 | tf_op jit(solution)/shard_map/ppermute | solution.py:8
  217.4 50.9 %collective-permute-start.3 = (f32[1024,128]{0,1:T(8,128)S(1)}, f32[1024,128]{0,1:T(8,128)S(1)}, u32[]{:S(2)}, u32[]{:S(2)}) collective-permute-start(f32[1024,128]{0,1:T(8,128)S(1)} %pad_maximum_fusion.7), channel_id=1, source_target_pairs={{0,8},{1,9},{2,10},{3,11},{4,12},{5,13},{6,14},{7,15},{8,0},{9,1},... | collective-permute-start | bytes 1572872 | tf_op jit(solution)/shard_map/ppermute | solution.py:8
